TPU v7x, 256 devices: a whole 4x4x8 slice. The times are simulated.
256 devices in a mesh: strip: 16 (over z, y_hi), chan: 16 (over y_lo, x, core).
Axes of the slice: x: 4, y: 4 (y_hi: 2, y_lo: 2; y = y_hi * 2 + y_lo), z: 8, core: 2. Of those that a mesh axis runs over, the one named last changes fastest.
Arguments:
- grid: bfloat16 [2, 64, 1024, 1024], P(None, 'chan', 'strip'), may hold values from -6 to 6
- model_image: float32 [64, 1024, 1024], P('chan', 'strip'), may hold values from -160 to 160
- step_size: float32 [64], P('chan'), may hold values from 0.5 to 1.5
- highpass: float32 [3, 4], replicated, may hold values from -1.4 to 1.4
- shrinkage: float32 [16], P('strip'), may hold values from 0.1 to 0.5
Outputs:
- updated: float32 [64, 1024, 1024], P('chan', 'strip')
All inputs are finite; a program needn't handle non-finite values.
Results may differ from a plain program's by a relative error of at most 0.0019.
Values may be sent and summed in bfloat16 or wider, within the bound.
A program may use at most 64 MiB of HBM per device.

v0:
```python
import functools

import jax
import jax.numpy as jnp
import numpy as np
from jax import lax
from jax.experimental import pallas as pl
from jax.experimental.pallas import tpu as pltpu
from jax.sharding import PartitionSpec as P

NS_ITERS = 5
MESH = pl.DeviceIdType.MESH
HALO = 16
NT = (((1,), (1,)), ((), ()))
F32 = jnp.float32
BF16 = jnp.bfloat16


def make_tables(side, strips):
    index = np.arange(side, dtype=np.int64)
    phases = (index[:, None] * index[None, :] % side) * (2.0 * np.pi / side)
    scale = float(side) ** -0.5
    both = np.stack((np.cos(phases), np.sin(phases))) * scale
    return jnp.asarray(both.astype(np.float32)).astype(BF16).reshape(2, strips, side // strips, side)


def exact_dot(a, b):
    return jnp.dot(a, b, precision=lax.Precision.HIGHEST, preferred_element_type=F32)


def kernel(
    strips, chans, tab, grid, model, step, taps, shrink, out,
    tabn, pairs, g_v, m_v, xc, xs, send_a, recv_a, ext_hi, ext_lo, base, send_b, recv_b, x, grecv,
    stage, send_c, polar,
    load_sem, tab_sem, a_send, a_recv, b_send, b_recv, g_send, g_recv, c_send, c_recv, h_send, h_recv,
):
    me_s = lax.axis_index("strip")
    me_c = lax.axis_index("chan")
    local, rows, side = base.shape
    wide = 2 * rows
    half = rows // 2
    lb = me_c // 2
    rh = lax.rem(me_c, 2)
    levels, filt = taps.shape

    def strip_peer(d):
        return lax.rem(me_s + d + strips, strips)

    def chan_peer(d):
        return lax.rem(me_c + d + chans, chans)

    load_grid = pltpu.make_async_copy(grid, g_v, load_sem.at[0])
    load_grid.start()
    load_model = pltpu.make_async_copy(model, m_v, load_sem.at[1])
    load_model.start()
    nblk = strips // 4
    first = me_s // 4

    def block_of(i):
        return lax.rem(first + i, nblk) * 4

    def tab_copy(i, r):
        rows_of = pl.ds(block_of(i), 4)
        return pltpu.make_async_copy(tab.at[r, rows_of], tabn.at[r, rows_of], tab_sem.at[i, r])

    for i in range(nblk):
        for r in range(2):
            tab_copy(i, r).start()
    load_pairs = [pltpu.make_async_copy(tab.at[r], pairs.at[:, r], load_sem.at[2 + r]) for r in range(2)]
    for cp in load_pairs:
        cp.start()

    barrier = pltpu.get_barrier_semaphore()

    @pl.loop(1, strips)
    def _(d):
        pl.semaphore_signal(barrier, inc=1, device_id=(strip_peer(d), me_c), device_id_type=MESH)

    @pl.loop(1, chans)
    def _(d):
        pl.semaphore_signal(barrier, inc=1, device_id=(me_s, chan_peer(d)), device_id_type=MESH)

    load_model.wait()
    ext_hi[:, rows + 2 * HALO :, :] = jnp.zeros((local, 128 - rows - 2 * HALO, side), BF16)
    ext_lo[:, :HALO, :] = jnp.zeros((local, HALO, side), BF16)
    ext_lo[:, rows + HALO :, :] = jnp.zeros((local, 128 - rows - HALO, side), BF16)
    for c in range(local):
        value = m_v[c]
        top = value.astype(BF16)
        ext_hi[c, HALO : HALO + rows, :] = top
        ext_lo[c, HALO : HALO + rows, :] = (value - top.astype(F32)).astype(BF16)

    load_grid.wait()
    for c in range(local):
        re = g_v[0, c]
        im = -g_v[1, c]
        xc[c * wide : c * wide + rows, :] = re
        xc[c * wide + rows : (c + 1) * wide, :] = im
        xs[c * wide : c * wide + rows, :] = im
        xs[c * wide + rows : (c + 1) * wide, :] = -re

    pl.semaphore_wait(barrier, strips - 1 + chans - 1)

    halo_copies = [
        pltpu.make_async_remote_copy(
            src_ref=ext_hi.at[:, rows : rows + HALO, :], dst_ref=ext_hi.at[:, 0:HALO, :],
            send_sem=h_send.at[0], recv_sem=h_recv.at[0],
            device_id=(strip_peer(1), me_c), device_id_type=MESH,
        ),
        pltpu.make_async_remote_copy(
            src_ref=ext_hi.at[:, HALO : 2 * HALO, :], dst_ref=ext_hi.at[:, rows + HALO : rows + 2 * HALO, :],
            send_sem=h_send.at[1], recv_sem=h_recv.at[1],
            device_id=(strip_peer(-1), me_c), device_id_type=MESH,
        ),
    ]
    for cp in halo_copies:
        cp.start()

    def a_src(k, d):
        return send_a.at[pl.ds(pl.multiple_of(strip_peer(d) * rows, rows), rows), pl.ds(k * wide, wide)]

    def a_dst(k):
        return recv_a.at[k, :, pl.ds(pl.multiple_of(me_s * wide, wide), wide)]

    def a_remote(k, d):
        return pltpu.make_async_remote_copy(
            src_ref=a_src(k, d), dst_ref=a_dst(k), send_sem=a_send.at[k, d], recv_sem=a_recv.at[k, d],
            device_id=(strip_peer(d), me_c), device_id_type=MESH,
        )

    def a_local(k):
        return pltpu.make_async_copy(a_src(k, 0), a_dst(k), a_recv.at[k, 0])

    @pl.loop(0, nblk)
    def _(i):
        b = block_of(i)
        for r in range(2):
            tab_copy(i, r).wait()
        cos_rows = tabn[0, pl.ds(b, 4)].reshape(4 * rows, side)
        sin_rows = tabn[1, pl.ds(b, 4)].reshape(4 * rows, side)
        value = lax.dot_general(cos_rows, xc[...], NT, preferred_element_type=F32)
        value = value + lax.dot_general(sin_rows, xs[...], NT, preferred_element_type=F32)
        send_a[pl.ds(pl.multiple_of(b * rows, 4 * rows), 4 * rows), :] = value.astype(BF16)

        @pl.loop(0, 4)
        def _(t):
            d = lax.rem(b + t - me_s + strips, strips)

            @pl.when(d != 0)
            def _():
                a_remote(0, d).start()

            @pl.when(d == 0)
            def _():
                a_local(0).start()

    for k in range(1, local):
        a_local(k).start()

        @pl.loop(1, strips)
        def _(d):
            a_remote(k, d).start()

    row = lax.broadcasted_iota(jnp.int32, (rows, 128), 0)
    col = lax.broadcasted_iota(jnp.int32, (rows, 128), 1)
    shift = col - row - HALO
    total = strips * rows
    base_row = me_s * rows
    band = jnp.zeros((rows, 128), F32)
    for j in range(levels):
        dil = 2**j
        for k in range(filt):
            inner = jnp.zeros((rows, 128), F32)
            for q in range(filt):
                inner = inner + jnp.where(shift == (q - k) * dil, taps[j, q], 0.0)
            detail_row = base_row + row - (k - filt // 2) * dil
            ok = jnp.logical_and(detail_row >= 0, detail_row < total)
            band = band + jnp.where(ok, taps[j, k] * inner, 0.0)
    image_row = base_row + col - HALO
    band = jnp.where(jnp.logical_and(image_row >= 0, image_row < total), band, 0.0)
    band_hi = band.astype(BF16)
    band_lo = (band - band_hi.astype(F32)).astype(BF16)
    x[...] = jnp.zeros(x.shape, BF16)
    for cp in halo_copies:
        cp.wait_recv()
    for c in range(local):
        near = ext_hi[c]
        wav = jnp.dot(band_hi, near, preferred_element_type=F32)
        wav = wav + jnp.dot(band_hi, ext_lo[c], preferred_element_type=F32)
        wav = wav + jnp.dot(band_lo, near, preferred_element_type=F32)
        base[c] = m_v[c] - step[c] * wav

    for cp in load_pairs:
        cp.wait()

    def b_remote(k, d):
        peer = chan_peer(d)
        return pltpu.make_async_remote_copy(
            src_ref=send_b.at[
                k, pl.ds(pl.multiple_of(lax.rem(peer, 2) * half, half), half), pl.ds(pl.multiple_of(peer // 2 * 128, 128), 128)
            ],
            dst_ref=recv_b.at[k, me_c], send_sem=b_send.at[k, d], recv_sem=b_recv.at[k, d],
            device_id=(me_s, peer), device_id_type=MESH,
        )

    def b_local(k):
        return pltpu.make_async_copy(
            send_b.at[k, pl.ds(pl.multiple_of(rh * half, half), half), pl.ds(pl.multiple_of(lb * 128, 128), 128)],
            recv_b.at[k, me_c], b_recv.at[k, 0],
        )

    def arrive_a(k):
        a_local(k).wait()

        @pl.loop(1, strips)
        def _(d):
            a_remote(k, d).wait_recv()

        @pl.loop(0, side // 256)
        def _(n):
            cols = pl.ds(pl.multiple_of(n * 256, 256), 256)
            dirty = jnp.dot(
                recv_a[k], pairs[:, :, :, cols].reshape(strips * wide, 256), preferred_element_type=F32
            )
            value = base[k, :, cols] + step[k] * dirty
            base[k, :, cols] = value
            send_b[k, :, cols] = value.astype(BF16)

        b_local(k).start()

        @pl.loop(1, chans)
        def _(d):
            b_remote(k, d).start()

    def g_remote(k, d):
        return pltpu.make_async_remote_copy(
            src_ref=grecv.at[k, me_c], dst_ref=grecv.at[k, me_c], send_sem=g_send.at[k, d], recv_sem=g_recv.at[k, d],
            device_id=(me_s, chan_peer(d)), device_id_type=MESH,
        )

    def arrive_b(k):
        b_local(k).wait()

        @pl.loop(1, chans)
        def _(d):
            b_remote(k, d).wait_recv()

        stage[: chans * half, :] = recv_b[k].astype(F32).reshape(chans * half, 128)
        for m in range(half):
            x[k * chans : (k + 1) * chans, m * 128 : (m + 1) * 128] = stage[pl.ds(m, chans, stride=half), :].astype(BF16)
        part = lax.dot_general(x[k * chans : (k + 1) * chans, :], x[...], NT, preferred_element_type=F32)
        grecv[k, me_c] = part

        @pl.loop(1, chans)
        def _(d):
            g_remote(k, d).start()

    for k in range(local):
        arrive_a(k)
        if k:
            arrive_b(k - 1)
    arrive_b(local - 1)

    size = local * chans
    blocks = []
    for k in range(local):

        @pl.loop(1, chans)
        def _(d):
            g_remote(k, d).wait_recv()

        blocks.append(jnp.sum(grecv[k], axis=0))
    low = jnp.concatenate(blocks, axis=0)[:, :size]
    gi = lax.broadcasted_iota(jnp.int32, (size, size), 0)
    gj = lax.broadcasted_iota(jnp.int32, (size, size), 1)
    identity = jnp.where(gi == gj, 1.0, 0.0).astype(F32)
    strict = jnp.where(gi // chans > gj // chans, low, 0.0)
    upper = lax.dot_general(
        strict, identity, (((0,), (0,)), ((), ())), precision=lax.Precision.HIGHEST, preferred_element_type=F32
    )
    gram = low + upper
    square = jnp.sum(jnp.sum(gram * gram, axis=1, keepdims=True), axis=0, keepdims=True)
    frob = jnp.sqrt(square)
    current = gram / frob
    inverse = 0.5 * (3.0 * identity - current)
    current = exact_dot(current, inverse)
    for it in range(1, NS_ITERS):
        middle = 0.5 * (3.0 * identity - exact_dot(inverse, current))
        if it + 1 < NS_ITERS:
            current = exact_dot(current, middle)
        inverse = exact_dot(middle, inverse)
    factor = shrink[0] * jnp.sqrt(float(rows * side) / frob)
    mix = lax.dot_general(
        inverse, identity, (((0,), (0,)), ((), ())), precision=lax.Precision.HIGHEST, preferred_element_type=F32
    )
    mix = (factor * mix).astype(BF16)

    for q in range(half // 4):
        value = jnp.dot(mix, x[:size, q * 512 : (q + 1) * 512], preferred_element_type=F32)
        for t in range(4):
            stage[pl.ds(q * 4 + t, size, stride=half), :] = value[:, t * 128 : (t + 1) * 128]
    for k in range(local):
        span = chans * half
        send_c[:, k] = stage[k * span : (k + 1) * span, :].reshape(chans, half, 128).astype(BF16)

    def c_dst():
        return polar.at[:, pl.ds(pl.multiple_of(rh * half, half), half), pl.ds(pl.multiple_of(lb * 128, 128), 128)]

    def c_remote(d):
        peer = chan_peer(d)
        return pltpu.make_async_remote_copy(
            src_ref=send_c.at[peer], dst_ref=c_dst(), send_sem=c_send.at[d], recv_sem=c_recv.at[d],
            device_id=(me_s, peer), device_id_type=MESH,
        )

    own = pltpu.make_async_copy(send_c.at[me_c], c_dst(), c_recv.at[0])
    own.start()

    @pl.loop(1, chans)
    def _(d):
        c_remote(d).start()

    own.wait()

    @pl.loop(1, chans)
    def _(d):
        c_remote(d).wait_recv()

    for c in range(local):
        out[c] = base[c] - polar[c].astype(F32)

    for cp in halo_copies:
        cp.wait_send()
    for k in range(local):

        @pl.loop(1, strips)
        def _(d):
            a_remote(k, d).wait_send()

        @pl.loop(1, chans)
        def _(d):
            b_remote(k, d).wait_send()
            g_remote(k, d).wait_send()

    @pl.loop(1, chans)
    def _(d):
        c_remote(d).wait_send()


def solution(mesh):
    strips, chans = mesh.shape["strip"], mesh.shape["chan"]

    def step_fn(grid, model, step, taps, shrink):
        local, rows, side = model.shape
        wide = 2 * rows
        half = rows // 2
        tab = make_tables(side, strips)
        dma = pltpu.SemaphoreType.DMA
        anywhere = pl.BlockSpec(memory_space=pl.ANY)
        scalars = pl.BlockSpec(memory_space=pltpu.SMEM)
        return pl.pallas_call(
            functools.partial(kernel, strips, chans),
            out_shape=jax.ShapeDtypeStruct((local, rows, side), F32),
            in_specs=[anywhere, anywhere, anywhere, scalars, scalars, scalars],
            out_specs=pl.BlockSpec(memory_space=pltpu.VMEM),
            scratch_shapes=[
                pltpu.VMEM((2, strips, rows, side), BF16),
                pltpu.VMEM((strips, 2, rows, side), BF16),
                pltpu.VMEM((2, local, rows, side), BF16),
                pltpu.VMEM((local, rows, side), F32),
                pltpu.VMEM((local * wide, side), BF16),
                pltpu.VMEM((local * wide, side), BF16),
                pltpu.VMEM((side, local * wide), BF16),
                pltpu.VMEM((local, rows, strips * wide), BF16),
                pltpu.VMEM((local, 128, side), BF16),
                pltpu.VMEM((local, 128, side), BF16),
                pltpu.VMEM((local, rows, side), F32),
                pltpu.VMEM((local, rows, side), BF16),
                pltpu.VMEM((local, chans, half, 128), BF16),
                pltpu.VMEM((128, half * 128), BF16),
                pltpu.VMEM((local, chans, chans, 128), F32),
                pltpu.VMEM((local * chans * half, 128), F32),
                pltpu.VMEM((chans, local, half, 128), BF16),
                pltpu.VMEM((local, rows, side), BF16),
                dma((4,)), dma((strips // 4, 2)),
                dma((local, strips)), dma((local, strips)),
                dma((local, chans)), dma((local, chans)),
                dma((local, chans)), dma((local, chans)),
                dma((chans,)), dma((chans,)),
                dma((2,)), dma((2,)),
            ],
            compiler_params=pltpu.CompilerParams(
                collective_id=0, has_side_effects=True, vmem_limit_bytes=62 * 1024 * 1024
            ),
            name="imaging_step",
        )(tab, grid, model, step, taps, shrink)

    return jax.shard_map(
        step_fn,
        mesh=mesh,
        in_specs=(
            P(None, "chan", "strip", None),
            P("chan", "strip", None),
            P("chan"),
            P(),
            P("strip"),
        ),
        out_specs=P("chan", "strip", None),
        check_vma=False,
    )
```

profile of v0, /device:TPU:1, one launch (start us, length us, event | category | flops | bytes accessed | tf_op | source)
XLA Modules:
  0.0 71.6 jit_solution(13214644973115987319)
XLA Ops:
  0.7 68.7 %imaging_step.1 = f32[4,64,1024]{2,1,0:T(8,128)} custom-call(bf16[2,16,64,1024]{3,2,1,0:T(8,128)(2,1)} %constant.8.tab, bf16[2,4,64,1024]{3,2,1,0:T(8,128)(2,1)} %grid.1, f32[4,64,1024]{2,1,0:T(8,128)} %model.1, f32[4]{0:T(128)} %step.1, f32[3,4]{1,0:T(4,128)} %taps.1, f32[1]{0:T(128)S(6)} %copy.8.shrink), custom_call_target="tpu_custom_call" | custom-call | tf_op jit(solution)/shard_map/imaging_step/pallas_call | solution.py:361
  69.3 2.3 %copy.9 = f32[4,64,1024]{2,1,0:T(8,128)} copy(f32[4,64,1024]{2,1,0:T(8,128)} %imaging_step.1) | data formatting | bytes 2097152
where the time goes:
time: 71.8 us; the launch traced here: 71.6 us
  Pallas kernels  68.7 us (96%)
  local copies, waits for them, and re-layouts  2.31 us (3%)
    pallas_call x1, Pallas kernels, step_fn(): pl.pallas_call(functools.partial(kernel, strips, chans), out_shape=jax.Sh...  68.7 us
    unnamed x1, local copies, waits for them, and re-layouts  2.31 us

commit v1 on v0

v1 whole, which is shorter than its diff:
```python
import functools

import jax
import jax.numpy as jnp
import numpy as np
from jax import lax
from jax.experimental import pallas as pl
from jax.experimental.pallas import tpu as pltpu
from jax.sharding import PartitionSpec as P

NS_ITERS = 5
MESH = pl.DeviceIdType.MESH
HALO = 16
NT = (((1,), (1,)), ((), ()))
F32 = jnp.float32
BF16 = jnp.bfloat16


def make_tables(side, strips):
    index = np.arange(side, dtype=np.int64)
    phases = (index[:, None] * index[None, :] % side) * (2.0 * np.pi / side)
    scale = float(side) ** -0.5
    both = np.stack((np.cos(phases), np.sin(phases))) * scale
    both = both.reshape(2, strips, side // strips, side).swapaxes(0, 1)
    return jnp.asarray(both.astype(np.float32).astype(BF16))


def exact_dot(a, b):
    return jnp.dot(a, b, precision=lax.Precision.HIGHEST, preferred_element_type=F32)


def kernel(
    strips, chans, tab, grid, model, step, taps, shrink, out,
    tb, g_v, m_v, xc, xs, send_a, recv_a, ext_hi, ext_lo, base, send_b, recv_b, x, grecv,
    stage, send_c, polar,
    load_sem, tab_sem, a_send, a_recv, b_send, b_recv, g_send, g_recv, c_send, c_recv, h_send, h_recv,
):
    me_s = lax.axis_index("strip")
    me_c = lax.axis_index("chan")
    local, rows, side = base.shape
    wide = 2 * rows
    half = rows // 2
    lb = me_c // 2
    rh = lax.rem(me_c, 2)
    levels, filt = taps.shape
    ring = strips // 2
    xring = chans // 4

    def slot_strip(j):
        q = j // 2
        dz = ring // 2 + ((q + 1) // 2) * (1 - 2 * lax.rem(q, 2))
        z = lax.rem(me_s // 2 - dz + 2 * ring, ring)
        return z * 2 + lax.rem(lax.rem(me_s, 2) + 1 - lax.rem(j, 2), 2)

    def partner_slot(j):
        q = j // 2
        inner = jnp.logical_and(q > 0, q < ring - 1)
        return j + jnp.where(inner, 2 * (2 * lax.rem(q, 2) - 1), 0)

    def chan_peer(j):
        q = j // 4
        dx = xring // 2 + ((q + 1) // 2) * (1 - 2 * lax.rem(q, 2))
        core = lax.rem(lax.rem(me_c, 2) + 1 - lax.rem(j, 2), 2)
        xpos = lax.rem(lax.rem(me_c // 2, xring) + dx + xring, xring)
        pair = lax.rem(me_c // (2 * xring) + 1 - lax.rem(j // 2, 2), 2)
        return pair * 2 * xring + xpos * 2 + core

    def strip_next(d):
        return lax.rem(me_s + d + strips, strips)

    barrier = pltpu.get_barrier_semaphore()

    @pl.loop(0, strips - 1)
    def _(j):
        pl.semaphore_signal(barrier, inc=1, device_id=(slot_strip(j), me_c), device_id_type=MESH)

    load_grid = pltpu.make_async_copy(grid, g_v, load_sem.at[0])
    load_grid.start()

    def tab_start(i):
        @pl.loop(4 * i, 4 * i + 4)
        def _(j):
            pltpu.make_async_copy(tab.at[slot_strip(j)], tb.at[j], tab_sem.at[i]).start()

    def tab_wait(i):
        part = tb.at[4 * i : 4 * i + 4]
        pltpu.make_async_copy(part, part, tab_sem.at[i]).wait()

    tab_start(0)

    @pl.loop(0, chans - 1)
    def _(j):
        pl.semaphore_signal(barrier, inc=1, device_id=(me_s, chan_peer(j)), device_id_type=MESH)

    nblk = strips // 4
    for i in range(1, nblk):
        tab_start(i)
    load_model = pltpu.make_async_copy(model, m_v, load_sem.at[1])
    load_model.start()

    load_grid.wait()
    for c in range(local):
        re = g_v[0, c]
        im = -g_v[1, c]
        xc[c * wide : c * wide + rows, :] = re
        xc[c * wide + rows : (c + 1) * wide, :] = im
        xs[c * wide : c * wide + rows, :] = im
        xs[c * wide + rows : (c + 1) * wide, :] = -re

    def a_src(k, j):
        return send_a.at[pl.ds(pl.multiple_of(j * rows, rows), rows), pl.ds(k * wide, wide)]

    def a_dst(k, j):
        return recv_a.at[k, :, pl.ds(pl.multiple_of(partner_slot(j) * wide, wide), wide)]

    def a_remote(k, j):
        return pltpu.make_async_remote_copy(
            src_ref=a_src(k, j), dst_ref=a_dst(k, j), send_sem=a_send, recv_sem=a_recv.at[k, partner_slot(j) // 4],
            device_id=(slot_strip(j), me_c), device_id_type=MESH,
        )

    def a_local(k):
        last = strips - 1
        return pltpu.make_async_copy(a_src(k, last), a_dst(k, last), a_recv.at[k, nblk - 1])

    for i in range(nblk):
        tab_wait(i)
        cos_rows = tb[4 * i : 4 * i + 4, 0].reshape(4 * rows, side)
        sin_rows = tb[4 * i : 4 * i + 4, 1].reshape(4 * rows, side)
        value = lax.dot_general(cos_rows, xc[...], NT, preferred_element_type=F32)
        value = value + lax.dot_general(sin_rows, xs[...], NT, preferred_element_type=F32)
        send_a[4 * i * rows : 4 * (i + 1) * rows, :] = value.astype(BF16)
        if i == 0:
            pl.semaphore_wait(barrier, strips - 1 + chans - 1)

        @pl.loop(4 * i, min(4 * i + 4, strips - 1))
        def _(j):
            a_remote(0, j).start()

    a_local(0).start()

    load_model.wait()
    ext_hi[:, rows + 2 * HALO :, :] = jnp.zeros((local, 128 - rows - 2 * HALO, side), BF16)
    ext_lo[:, :HALO, :] = jnp.zeros((local, HALO, side), BF16)
    ext_lo[:, rows + HALO :, :] = jnp.zeros((local, 128 - rows - HALO, side), BF16)
    for c in range(local):
        value = m_v[c]
        top = value.astype(BF16)
        ext_hi[c, HALO : HALO + rows, :] = top
        ext_lo[c, HALO : HALO + rows, :] = (value - top.astype(F32)).astype(BF16)
    halo_copies = [
        pltpu.make_async_remote_copy(
            src_ref=ext_hi.at[:, rows : rows + HALO, :], dst_ref=ext_hi.at[:, 0:HALO, :],
            send_sem=h_send.at[0], recv_sem=h_recv.at[0],
            device_id=(strip_next(1), me_c), device_id_type=MESH,
        ),
        pltpu.make_async_remote_copy(
            src_ref=ext_hi.at[:, HALO : 2 * HALO, :], dst_ref=ext_hi.at[:, rows + HALO : rows + 2 * HALO, :],
            send_sem=h_send.at[1], recv_sem=h_recv.at[1],
            device_id=(strip_next(-1), me_c), device_id_type=MESH,
        ),
    ]
    for cp in halo_copies:
        cp.start()

    for k in range(1, local):

        @pl.loop(0, strips - 1)
        def _(j):
            a_remote(k, j).start()

        a_local(k).start()

    row = lax.broadcasted_iota(jnp.int32, (rows, 128), 0)
    col = lax.broadcasted_iota(jnp.int32, (rows, 128), 1)
    shift = col - row - HALO
    total = strips * rows
    base_row = me_s * rows
    band = jnp.zeros((rows, 128), F32)
    for j in range(levels):
        dil = 2**j
        for k in range(filt):
            inner = jnp.zeros((rows, 128), F32)
            for q in range(filt):
                inner = inner + jnp.where(shift == (q - k) * dil, taps[j, q], 0.0)
            detail_row = base_row + row - (k - filt // 2) * dil
            ok = jnp.logical_and(detail_row >= 0, detail_row < total)
            band = band + jnp.where(ok, taps[j, k] * inner, 0.0)
    image_row = base_row + col - HALO
    band = jnp.where(jnp.logical_and(image_row >= 0, image_row < total), band, 0.0)
    band_hi = band.astype(BF16)
    band_lo = (band - band_hi.astype(F32)).astype(BF16)
    x[...] = jnp.zeros(x.shape, BF16)
    for cp in halo_copies:
        cp.wait_recv()
    for c in range(local):
        near = ext_hi[c]
        wav = jnp.dot(band_hi, near, preferred_element_type=F32)
        wav = wav + jnp.dot(band_hi, ext_lo[c], preferred_element_type=F32)
        wav = wav + jnp.dot(band_lo, near, preferred_element_type=F32)
        base[c] = m_v[c] - step[c] * wav

    def b_src(k, peer):
        return send_b.at[
            k, pl.ds(pl.multiple_of(lax.rem(peer, 2) * half, half), half), pl.ds(pl.multiple_of(peer // 2 * 128, 128), 128)
        ]

    def b_remote(k, j):
        peer = chan_peer(j)
        return pltpu.make_async_remote_copy(
            src_ref=b_src(k, peer), dst_ref=recv_b.at[k, me_c], send_sem=b_send, recv_sem=b_recv.at[k],
            device_id=(me_s, peer), device_id_type=MESH,
        )

    def arrive_a(k):
        for g in range(nblk):
            span = 4 * wide
            part = recv_a.at[k, :, g * span : (g + 1) * span]
            pltpu.make_async_copy(part, part, a_recv.at[k, g]).wait()
            dirty = jnp.dot(
                recv_a[k, :, g * span : (g + 1) * span], tb[4 * g : 4 * g + 4].reshape(span, side),
                preferred_element_type=F32,
            )
            value = base[k] + step[k] * dirty
            base[k] = value
            if g == nblk - 1:
                send_b[k] = value.astype(BF16)

        @pl.loop(0, chans - 1)
        def _(j):
            b_remote(k, j).start()

        pltpu.make_async_copy(b_src(k, me_c), recv_b.at[k, me_c], b_recv.at[k]).start()

    def g_remote(k, j):
        return pltpu.make_async_remote_copy(
            src_ref=grecv.at[k, me_c], dst_ref=grecv.at[k, me_c], send_sem=g_send, recv_sem=g_recv.at[k],
            device_id=(me_s, chan_peer(j)), device_id_type=MESH,
        )

    def arrive_b(k):
        part = recv_b.at[k]
        pltpu.make_async_copy(part, part, b_recv.at[k]).wait()
        stage[: chans * half, :] = recv_b[k].astype(F32).reshape(chans * half, 128)
        for m in range(half):
            x[k * chans : (k + 1) * chans, m * 128 : (m + 1) * 128] = stage[pl.ds(m, chans, stride=half), :].astype(BF16)
        part = lax.dot_general(x[k * chans : (k + 1) * chans, :], x[...], NT, preferred_element_type=F32)
        grecv[k, me_c] = part

        @pl.loop(0, chans - 1)
        def _(j):
            g_remote(k, j).start()

    for k in range(local):
        arrive_a(k)
        if k:
            arrive_b(k - 1)
    arrive_b(local - 1)

    size = local * chans
    blocks = []
    for k in range(local):
        part = grecv.at[k, : chans - 1]
        pltpu.make_async_copy(part, part, g_recv.at[k]).wait()
        blocks.append(jnp.sum(grecv[k], axis=0))
    low = jnp.concatenate(blocks, axis=0)[:, :size]
    gi = lax.broadcasted_iota(jnp.int32, (size, size), 0)
    gj = lax.broadcasted_iota(jnp.int32, (size, size), 1)
    identity = jnp.where(gi == gj, 1.0, 0.0).astype(F32)
    strict = jnp.where(gi // chans > gj // chans, low, 0.0)
    upper = lax.dot_general(
        strict, identity, (((0,), (0,)), ((), ())), precision=lax.Precision.HIGHEST, preferred_element_type=F32
    )
    gram = low + upper
    square = jnp.sum(jnp.sum(gram * gram, axis=1, keepdims=True), axis=0, keepdims=True)
    frob = jnp.sqrt(square)
    current = gram / frob
    inverse = 0.5 * (3.0 * identity - current)
    current = exact_dot(current, inverse)
    for it in range(1, NS_ITERS):
        middle = 0.5 * (3.0 * identity - exact_dot(inverse, current))
        if it + 1 < NS_ITERS:
            current = exact_dot(current, middle)
        inverse = exact_dot(middle, inverse)
    factor = shrink[0] * jnp.sqrt(float(rows * side) / frob)
    mix = lax.dot_general(
        inverse, identity, (((0,), (0,)), ((), ())), precision=lax.Precision.HIGHEST, preferred_element_type=F32
    )
    mix = (factor * mix).astype(BF16)

    for q in range(half // 4):
        value = jnp.dot(mix, x[:size, q * 512 : (q + 1) * 512], preferred_element_type=F32)
        for t in range(4):
            stage[pl.ds(q * 4 + t, size, stride=half), :] = value[:, t * 128 : (t + 1) * 128]
    for k in range(local):
        span = chans * half
        send_c[:, k] = stage[k * span : (k + 1) * span, :].reshape(chans, half, 128).astype(BF16)

    mine = polar.at[:, pl.ds(pl.multiple_of(rh * half, half), half), pl.ds(pl.multiple_of(lb * 128, 128), 128)]

    @pl.loop(0, chans - 1)
    def _(j):
        peer = chan_peer(j)
        pltpu.make_async_remote_copy(
            src_ref=send_c.at[peer], dst_ref=mine, send_sem=c_send, recv_sem=c_recv,
            device_id=(me_s, peer), device_id_type=MESH,
        ).start()

    pltpu.make_async_copy(send_c.at[me_c], mine, c_recv).start()
    pltpu.make_async_copy(polar, polar, c_recv).wait()
    for c in range(local):
        out[c] = base[c] - polar[c].astype(F32)

    for cp in halo_copies:
        cp.wait_send()
    for ref, sem in (
        (send_a.at[: (strips - 1) * rows], a_send),
        (recv_b.at[:, : chans - 1], b_send),
        (grecv.at[:, : chans - 1], g_send),
        (send_c.at[: chans - 1], c_send),
    ):
        pltpu.make_async_copy(ref, ref, sem).wait()


def solution(mesh):
    strips, chans = mesh.shape["strip"], mesh.shape["chan"]

    def step_fn(grid, model, step, taps, shrink):
        local, rows, side = model.shape
        wide = 2 * rows
        half = rows // 2
        tab = make_tables(side, strips)
        dma = pltpu.SemaphoreType.DMA
        anywhere = pl.BlockSpec(memory_space=pl.ANY)
        scalars = pl.BlockSpec(memory_space=pltpu.SMEM)
        return pl.pallas_call(
            functools.partial(kernel, strips, chans),
            out_shape=jax.ShapeDtypeStruct((local, rows, side), F32),
            in_specs=[anywhere, anywhere, anywhere, scalars, scalars, scalars],
            out_specs=pl.BlockSpec(memory_space=pltpu.VMEM),
            scratch_shapes=[
                pltpu.VMEM((strips, 2, rows, side), BF16),
                pltpu.VMEM((2, local, rows, side), BF16),
                pltpu.VMEM((local, rows, side), F32),
                pltpu.VMEM((local * wide, side), BF16),
                pltpu.VMEM((local * wide, side), BF16),
                pltpu.VMEM((side, local * wide), BF16),
                pltpu.VMEM((local, rows, strips * wide), BF16),
                pltpu.VMEM((local, 128, side), BF16),
                pltpu.VMEM((local, 128, side), BF16),
                pltpu.VMEM((local, rows, side), F32),
                pltpu.VMEM((local, rows, side), BF16),
                pltpu.VMEM((local, chans, half, 128), BF16),
                pltpu.VMEM((128, half * 128), BF16),
                pltpu.VMEM((local, chans, chans, 128), F32),
                pltpu.VMEM((local * chans * half, 128), F32),
                pltpu.VMEM((chans, local, half, 128), BF16),
                pltpu.VMEM((local, rows, side), BF16),
                dma((2,)), dma((strips // 4,)),
                dma, dma((local, strips // 4)),
                dma, dma((local,)),
                dma, dma((local,)),
                dma, dma,
                dma((2,)), dma((2,)),
            ],
            compiler_params=pltpu.CompilerParams(
                collective_id=0, has_side_effects=True, vmem_limit_bytes=62 * 1024 * 1024
            ),
            name="imaging_step",
        )(tab, grid, model, step, taps, shrink)

    return jax.shard_map(
        step_fn,
        mesh=mesh,
        in_specs=(
            P(None, "chan", "strip", None),
            P("chan", "strip", None),
            P("chan"),
            P(),
            P("strip"),
        ),
        out_specs=P("chan", "strip", None),
        check_vma=False,
    )
```

time: 71.8 us -> 66.7 us (0.929)
  Pallas kernels: 68.7 us -> 63.6 us
    pallas_call x1, Pallas kernels: 68.7 us -> 63.6 us  [step_fn(): pl.pallas_call(functools.partial(kernel, strips, chans), out_shape=jax.Sh...]
where the time goes in v1:
time: 66.7 us; the launch traced here: 66.6 us
  Pallas kernels  63.6 us (95%)
  local copies, waits for them, and re-layouts  2.31 us (3%)
    pallas_call x1, Pallas kernels, step_fn(): pl.pallas_call(functools.partial(kernel, strips, chans), out_shape=jax.Sh...  63.6 us
    unnamed x1, local copies, waits for them, and re-layouts  2.31 us

profile of v1, /device:TPU:1, one launch (start us, length us, event | category | flops | bytes accessed | tf_op | source)
XLA Modules:
  0.0 66.6 jit_solution(10143008843091115156)
XLA Ops:
  0.7 63.6 %imaging_step.1 = f32[4,64,1024]{2,1,0:T(8,128)} custom-call(bf16[16,2,64,1024]{3,2,1,0:T(8,128)(2,1)} %constant.2.clone.tab, bf16[2,4,64,1024]{3,2,1,0:T(8,128)(2,1)} %grid.1, f32[4,64,1024]{2,1,0:T(8,128)} %model.1, f32[4]{0:T(128)} %step.1, f32[3,4]{1,0:T(4,128)} %taps.1, f32[1]{0:T(128)S(6)} %copy.8.shrink), custom_call_target="tpu_custom_call" | custom-call | tf_op jit(solution)/shard_map/imaging_step/pallas_call | solution.py:336
  64.3 2.3 %copy.9 = f32[4,64,1024]{2,1,0:T(8,128)} copy(f32[4,64,1024]{2,1,0:T(8,128)} %imaging_step.1) | data formatting | bytes 2097152

commit v2 on v1

v2 whole, which is shorter than its diff:
```python
import functools

import jax
import jax.numpy as jnp
import numpy as np
from jax import lax
from jax.experimental import pallas as pl
from jax.experimental.pallas import tpu as pltpu
from jax.sharding import PartitionSpec as P

NS_ITERS = 5
MESH = pl.DeviceIdType.MESH
HALO = 16
NT = (((1,), (1,)), ((), ()))
F32 = jnp.float32
BF16 = jnp.bfloat16


def make_tables(side, strips):
    index = np.arange(side, dtype=np.int64)
    phases = (index[:, None] * index[None, :] % side) * (2.0 * np.pi / side)
    scale = float(side) ** -0.5
    both = np.stack((np.cos(phases), np.sin(phases))) * scale
    both = both.reshape(2, strips, side // strips, side).swapaxes(0, 1)
    return jnp.asarray(both.astype(np.float32).astype(BF16))


def split(a):
    high = a.astype(BF16)
    return high, (a - high.astype(F32)).astype(BF16)


def split_dot(a, b):
    out = jnp.dot(a[0], b[1], preferred_element_type=F32) + jnp.dot(a[1], b[0], preferred_element_type=F32)
    return out + jnp.dot(a[0], b[0], preferred_element_type=F32)


def kernel(
    strips, chans, tab, grid, model, step, taps, shrink, moved, polar,
    tb, g_v, m_v, xc, xs, send_a, recv_a, ext_hi, ext_lo, base, send_b, recv_b, x, grecv,
    stage, send_c,
    load_sem, tab_sem, a_send, a_recv, b_send, b_recv, g_send, g_recv, c_send, c_recv, h_send, h_recv, out_sem,
):
    me_s = lax.axis_index("strip")
    me_c = lax.axis_index("chan")
    local, rows, side = base.shape
    wide = 2 * rows
    half = rows // 2
    lb = me_c // 2
    rh = lax.rem(me_c, 2)
    levels, filt = taps.shape
    ring = strips // 2
    xring = chans // 4

    z_of = [lax.rem(me_s // 2 + d, ring) * 2 for d in range(ring)]
    z_bit = [lax.rem(me_s, 2), 1 - lax.rem(me_s, 2)]
    steps = [(ring // 2 + ((q + 1) // 2) * (1 - 2 * (q % 2))) % ring for q in range(ring)]
    slots = [(-steps[j // 2] % ring, 1 - j % 2) for j in range(strips)]
    strip_of = [z_of[d] + z_bit[t] for d, t in slots]
    partner = [slots.index((-d % ring, t)) for d, t in slots]

    x_of = [lax.rem(me_c // 2 + d, xring) * 2 for d in range(xring)]
    c_bit = [lax.rem(me_c, 2), 1 - lax.rem(me_c, 2)]
    me_pair = me_c // (2 * xring)
    p_bit = [me_pair * (2 * xring), (1 - me_pair) * (2 * xring)]
    xsteps = [(xring // 2 + ((q + 1) // 2) * (1 - 2 * (q % 2))) % xring for q in range(xring)]
    peers = [p_bit[1 - j // 2 % 2] + x_of[xsteps[j // 4]] + c_bit[1 - j % 2] for j in range(chans - 1)]

    def strip_next(d):
        return lax.rem(me_s + d + strips, strips)

    barrier = pltpu.get_barrier_semaphore()

    for j in range(strips - 1):
        pl.semaphore_signal(barrier, inc=1, device_id=(strip_of[j], me_c), device_id_type=MESH)

    load_grid = pltpu.make_async_copy(grid, g_v, load_sem.at[0])
    load_grid.start()

    def tab_start(i):
        for j in range(4 * i, 4 * i + 4):
            pltpu.make_async_copy(tab.at[strip_of[j]], tb.at[j], tab_sem.at[i]).start()

    def tab_wait(i):
        part = tb.at[4 * i : 4 * i + 4]
        pltpu.make_async_copy(part, part, tab_sem.at[i]).wait()

    tab_start(0)

    for peer in peers:
        pl.semaphore_signal(barrier, inc=1, device_id=(me_s, peer), device_id_type=MESH)

    nblk = strips // 4
    for i in range(1, nblk):
        tab_start(i)
    load_model = pltpu.make_async_copy(model, m_v, load_sem.at[1])
    load_model.start()

    load_grid.wait()
    for c in range(local):
        re = g_v[0, c]
        im = -g_v[1, c]
        xc[c * wide : c * wide + rows, :] = re
        xc[c * wide + rows : (c + 1) * wide, :] = im
        xs[c * wide : c * wide + rows, :] = im
        xs[c * wide + rows : (c + 1) * wide, :] = -re

    def a_src(k, j):
        return send_a.at[j * rows : (j + 1) * rows, k * wide : (k + 1) * wide]

    def a_dst(k, j):
        return recv_a.at[k, :, partner[j] * wide : (partner[j] + 1) * wide]

    def a_remote(k, j):
        return pltpu.make_async_remote_copy(
            src_ref=a_src(k, j), dst_ref=a_dst(k, j), send_sem=a_send, recv_sem=a_recv.at[k, partner[j] // 4],
            device_id=(strip_of[j], me_c), device_id_type=MESH,
        )

    def a_local(k):
        last = strips - 1
        return pltpu.make_async_copy(a_src(k, last), a_dst(k, last), a_recv.at[k, nblk - 1])

    for i in range(nblk):
        tab_wait(i)
        cos_rows = tb[4 * i : 4 * i + 4, 0].reshape(4 * rows, side)
        sin_rows = tb[4 * i : 4 * i + 4, 1].reshape(4 * rows, side)
        value = lax.dot_general(cos_rows, xc[...], NT, preferred_element_type=F32)
        value = value + lax.dot_general(sin_rows, xs[...], NT, preferred_element_type=F32)
        send_a[4 * i * rows : 4 * (i + 1) * rows, :] = value.astype(BF16)
        if i == 0:
            pl.semaphore_wait(barrier, strips - 1 + chans - 1)

        for j in range(4 * i, min(4 * i + 4, strips - 1)):
            a_remote(0, j).start()

    a_local(0).start()

    load_model.wait()
    ext_hi[:, rows + 2 * HALO :, :] = jnp.zeros((local, 128 - rows - 2 * HALO, side), BF16)
    ext_lo[:, :HALO, :] = jnp.zeros((local, HALO, side), BF16)
    ext_lo[:, rows + HALO :, :] = jnp.zeros((local, 128 - rows - HALO, side), BF16)
    for c in range(local):
        value = m_v[c]
        top = value.astype(BF16)
        ext_hi[c, HALO : HALO + rows, :] = top
        ext_lo[c, HALO : HALO + rows, :] = (value - top.astype(F32)).astype(BF16)
    halo_copies = [
        pltpu.make_async_remote_copy(
            src_ref=ext_hi.at[:, rows : rows + HALO, :], dst_ref=ext_hi.at[:, 0:HALO, :],
            send_sem=h_send.at[0], recv_sem=h_recv.at[0],
            device_id=(strip_next(1), me_c), device_id_type=MESH,
        ),
        pltpu.make_async_remote_copy(
            src_ref=ext_hi.at[:, HALO : 2 * HALO, :], dst_ref=ext_hi.at[:, rows + HALO : rows + 2 * HALO, :],
            send_sem=h_send.at[1], recv_sem=h_recv.at[1],
            device_id=(strip_next(-1), me_c), device_id_type=MESH,
        ),
    ]
    for cp in halo_copies:
        cp.start()

    for k in range(1, local):
        for j in range(strips - 1):
            a_remote(k, j).start()

        a_local(k).start()

    row = lax.broadcasted_iota(jnp.int32, (rows, 128), 0)
    col = lax.broadcasted_iota(jnp.int32, (rows, 128), 1)
    shift = col - row - HALO
    total = strips * rows
    base_row = me_s * rows
    band = jnp.zeros((rows, 128), F32)
    for j in range(levels):
        dil = 2**j
        for k in range(filt):
            inner = jnp.zeros((rows, 128), F32)
            for q in range(filt):
                inner = inner + jnp.where(shift == (q - k) * dil, taps[j, q], 0.0)
            detail_row = base_row + row - (k - filt // 2) * dil
            ok = jnp.logical_and(detail_row >= 0, detail_row < total)
            band = band + jnp.where(ok, taps[j, k] * inner, 0.0)
    image_row = base_row + col - HALO
    band = jnp.where(jnp.logical_and(image_row >= 0, image_row < total), band, 0.0)
    band_hi = band.astype(BF16)
    band_lo = (band - band_hi.astype(F32)).astype(BF16)
    x[...] = jnp.zeros(x.shape, BF16)
    def b_src(k, peer):
        return send_b.at[
            k, pl.ds(pl.multiple_of(lax.rem(peer, 2) * half, half), half), pl.ds(pl.multiple_of(peer // 2 * 128, 128), 128)
        ]

    def b_remote(k, peer):
        return pltpu.make_async_remote_copy(
            src_ref=b_src(k, peer), dst_ref=recv_b.at[k, me_c], send_sem=b_send, recv_sem=b_recv.at[k],
            device_id=(me_s, peer), device_id_type=MESH,
        )

    def wavelet():
        for cp in halo_copies:
            cp.wait_recv()
        for c in range(local):
            near = ext_hi[c]
            wav = jnp.dot(band_hi, near, preferred_element_type=F32)
            wav = wav + jnp.dot(band_hi, ext_lo[c], preferred_element_type=F32)
            wav = wav + jnp.dot(band_lo, near, preferred_element_type=F32)
            m_v[c] = m_v[c] - step[c] * wav

    def arrive_a(k):
        for g in range(nblk):
            span = 4 * wide
            part = recv_a.at[k, :, g * span : (g + 1) * span]
            pltpu.make_async_copy(part, part, a_recv.at[k, g]).wait()
            dirty = jnp.dot(
                recv_a[k, :, g * span : (g + 1) * span], tb[4 * g : 4 * g + 4].reshape(span, side),
                preferred_element_type=F32,
            )
            base[k] = base[k] + dirty if g else dirty

    def depart_b(k):
        value = m_v[k] + step[k] * base[k]
        base[k] = value
        send_b[k] = value.astype(BF16)

        for peer in peers:
            b_remote(k, peer).start()

        pltpu.make_async_copy(b_src(k, me_c), recv_b.at[k, me_c], b_recv.at[k]).start()
        pltpu.make_async_copy(base.at[k], moved.at[k], out_sem).start()

    def g_remote(k, peer):
        return pltpu.make_async_remote_copy(
            src_ref=grecv.at[k, me_c], dst_ref=grecv.at[k, me_c], send_sem=g_send, recv_sem=g_recv.at[k],
            device_id=(me_s, peer), device_id_type=MESH,
        )

    def arrive_b(k):
        part = recv_b.at[k]
        pltpu.make_async_copy(part, part, b_recv.at[k]).wait()
        stage[: chans * half, :] = recv_b[k].astype(F32).reshape(chans * half, 128)
        for m in range(half):
            x[k * chans : (k + 1) * chans, m * 128 : (m + 1) * 128] = stage[pl.ds(m, chans, stride=half), :].astype(BF16)
        part = lax.dot_general(x[k * chans : (k + 1) * chans, :], x[...], NT, preferred_element_type=F32)
        grecv[k, me_c] = part[: chans // 2] + pltpu.roll(part[chans // 2 :], size, 1)

        for peer in peers:
            g_remote(k, peer).start()

    last = local - 1
    size = local * chans
    for k in range(last):
        arrive_a(k)
        if k == 1:
            wavelet()
            depart_b(0)
        if k:
            depart_b(k)
    for k in range(last - 1):
        arrive_b(k)
    arrive_a(last)
    depart_b(last)
    arrive_b(last - 1)
    arrive_b(last)

    blocks = []
    for k in range(local):
        part = grecv.at[k, : chans - 1]
        pltpu.make_async_copy(part, part, g_recv.at[k]).wait()
        part = jnp.sum(grecv[k], axis=0)
        blocks += [part, pltpu.roll(part, size, 1)]
    low = jnp.concatenate(blocks, axis=0)[:, :size]
    gi = lax.broadcasted_iota(jnp.int32, (size, size), 0)
    gj = lax.broadcasted_iota(jnp.int32, (size, size), 1)
    identity = jnp.where(gi == gj, 1.0, 0.0).astype(F32)
    strict = jnp.where(gi // chans > gj // chans, low, 0.0)
    upper = lax.dot_general(
        strict, identity, (((0,), (0,)), ((), ())), precision=lax.Precision.HIGHEST, preferred_element_type=F32
    )
    gram = low + upper
    square = jnp.sum(jnp.sum(gram * gram, axis=1, keepdims=True), axis=0, keepdims=True)
    frob = jnp.sqrt(square)
    current = gram / frob
    inverse = 0.5 * (3.0 * identity - current)
    current = split_dot(split(current), split(inverse))
    for it in range(1, NS_ITERS):
        parts = split(inverse)
        halves = split(current)
        middle = split(0.5 * (3.0 * identity - split_dot(parts, halves)))
        if it + 1 < NS_ITERS:
            current = split_dot(halves, middle)
        inverse = split_dot(middle, parts)
    mix = (shrink[0] * jnp.sqrt(float(rows * side) / frob) * inverse).astype(BF16)

    quarter = half // 2
    span = chans * quarter
    for h in range(2):
        for q in range(quarter // 4):
            first = (h * quarter + q * 4) * 128
            value = jnp.dot(mix, x[:size, first : first + 512], preferred_element_type=F32)
            for t in range(4):
                stage[pl.ds(q * 4 + t, size, stride=quarter), :] = value[:, t * 128 : (t + 1) * 128]
        for k in range(local):
            send_c[h, :, k] = stage[k * span : (k + 1) * span, :].reshape(chans, quarter, 128).astype(BF16)
        mine = polar.at[
            :, pl.ds(pl.multiple_of(rh * half + h * quarter, quarter), quarter), pl.ds(pl.multiple_of(lb * 128, 128), 128)
        ]

        for peer in peers:
            pltpu.make_async_remote_copy(
                src_ref=send_c.at[h, peer], dst_ref=mine, send_sem=c_send, recv_sem=c_recv,
                device_id=(me_s, peer), device_id_type=MESH,
            ).start()

        pltpu.make_async_copy(send_c.at[h, me_c], mine, c_recv).start()
    pltpu.make_async_copy(base, moved, out_sem).wait()
    pltpu.make_async_copy(polar, polar, c_recv).wait()

    for cp in halo_copies:
        cp.wait_send()
    for ref, sem in (
        (send_a.at[: (strips - 1) * rows], a_send),
        (recv_b.at[:, : chans - 1], b_send),
        (grecv.at[:, : chans - 1], g_send),
        (send_c.at[:, : chans - 1], c_send),
    ):
        pltpu.make_async_copy(ref, ref, sem).wait()


def solution(mesh):
    strips, chans = mesh.shape["strip"], mesh.shape["chan"]

    def step_fn(grid, model, step, taps, shrink):
        local, rows, side = model.shape
        wide = 2 * rows
        half = rows // 2
        tab = make_tables(side, strips)
        dma = pltpu.SemaphoreType.DMA
        anywhere = pl.BlockSpec(memory_space=pl.ANY)
        scalars = pl.BlockSpec(memory_space=pltpu.SMEM)
        moved, polar = pl.pallas_call(
            functools.partial(kernel, strips, chans),
            out_shape=(
                pltpu.VMEM((local, rows, side), F32),
                pltpu.VMEM((local, rows, side), BF16),
            ),
            in_specs=[anywhere, anywhere, anywhere, scalars, scalars, scalars],
            out_specs=(pl.BlockSpec(memory_space=pltpu.VMEM),) * 2,
            scratch_shapes=[
                pltpu.VMEM((strips, 2, rows, side), BF16),
                pltpu.VMEM((2, local, rows, side), BF16),
                pltpu.VMEM((local, rows, side), F32),
                pltpu.VMEM((local * wide, side), BF16),
                pltpu.VMEM((local * wide, side), BF16),
                pltpu.VMEM((side, local * wide), BF16),
                pltpu.VMEM((local, rows, strips * wide), BF16),
                pltpu.VMEM((local, 128, side), BF16),
                pltpu.VMEM((local, 128, side), BF16),
                pltpu.VMEM((local, rows, side), F32),
                pltpu.VMEM((local, rows, side), BF16),
                pltpu.VMEM((local, chans, half, 128), BF16),
                pltpu.VMEM((128, half * 128), BF16),
                pltpu.VMEM((local, chans, chans // 2, 128), F32),
                pltpu.VMEM((local * chans * half // 2, 128), F32),
                pltpu.VMEM((2, chans, local, half // 2, 128), BF16),
                dma((2,)), dma((strips // 4,)),
                dma, dma((local, strips // 4)),
                dma, dma((local,)),
                dma, dma((local,)),
                dma, dma,
                dma((2,)), dma((2,)), dma,
            ],
            compiler_params=pltpu.CompilerParams(
                collective_id=0, has_side_effects=True, vmem_limit_bytes=60 * 1024 * 1024
            ),
            name="imaging_step",
        )(tab, grid, model, step, taps, shrink)
        return moved - polar.astype(F32)

    return jax.shard_map(
        step_fn,
        mesh=mesh,
        in_specs=(
            P(None, "chan", "strip", None),
            P("chan", "strip", None),
            P("chan"),
            P(),
            P("strip"),
        ),
        out_specs=P("chan", "strip", None),
        check_vma=False,
    )
```

time: 66.7 us -> 61.6 us (0.924)
  Pallas kernels: 63.6 us -> 59.7 us
  local copies, waits for them, and re-layouts: 2.31 us -> 0 us
  other arithmetic: 0 us -> 1.16 us
    pallas_call x1, Pallas kernels: 63.6 us -> 59.7 us  [step_fn(): pl.pallas_call(functools.partial(kernel, strips, chans), out_shape=(pltpu...]
    unnamed x1 -> x0, local copies, waits for them, and re-layouts: 2.31 us -> none
    sub x0 -> x1, other arithmetic: none -> 1.16 us  [step_fn(): return moved - polar.astype(F32)]
where the time goes in v2:
time: 61.6 us; the launch traced here: 61.5 us
  Pallas kernels  59.7 us (97%)
  other arithmetic  1.16 us (2%)
  between operations  0.66 us (1%)
    pallas_call x1, Pallas kernels, step_fn(): pl.pallas_call(functools.partial(kernel, strips, chans), out_shape=(pltpu...  59.7 us

profile of v2, /device:TPU:1, one launch (start us, length us, event | category | flops | bytes accessed | tf_op | source)
XLA Modules:
  0.0 61.5 jit_solution(990201496543844889)
XLA Ops:
  0.7 59.7 %imaging_step.1 = (f32[4,64,1024]{2,1,0:T(8,128)S(1)}, bf16[4,64,1024]{2,1,0:T(8,128)(2,1)S(1)}) custom-call(bf16[16,2,64,1024]{3,2,1,0:T(8,128)(2,1)} %constant.2.clone.tab, bf16[2,4,64,1024]{3,2,1,0:T(8,128)(2,1)} %grid.1, f32[4,64,1024]{2,1,0:T(8,128)} %model.1, f32[4]{0:T(128)} %step.1, f32[3,4]{1,0:T(4,128)} %taps.1, f32[1]{0:T(128)S(6)} %copy.7.shrink), custom_call_target="tpu_custom_call" | custom-call | tf_op jit(solution)/shard_map/imaging_step/pallas_call | solution.py:341
  60.4 1.2 %convert_subtract_fusion = f32[4,64,1024]{2,1,0:T(8,128)} fusion(f32[4,64,1024]{2,1,0:T(8,128)S(1)} %get-tuple-element.7, bf16[4,64,1024]{2,1,0:T(8,128)(2,1)S(1)} %get-tuple-element.8), kind=kLoop, calls=%fused_computation | loop fusion | flops 524288 | bytes 2621440 | tf_op jit(solution)/shard_map/sub | solution.py:378

commit v3 on v2

--- a/solution.py
+++ b/solution.py
@@ -10,7 +10,6 @@
 
 NS_ITERS = 5
 MESH = pl.DeviceIdType.MESH
-HALO = 16
 NT = (((1,), (1,)), ((), ()))
 F32 = jnp.float32
 BF16 = jnp.bfloat16
@@ -37,8 +36,8 @@
 
 def kernel(
     strips, chans, tab, grid, model, step, taps, shrink, moved, polar,
-    tb, g_v, m_v, xc, xs, send_a, recv_a, ext_hi, ext_lo, base, send_b, recv_b, x, grecv,
-    stage, send_c,
+    tb, g_v, m_v, xc, xs, send_a, recv_a, own_hi, own_lo, base, send_b, recv_b, x, grecv,
+    stage, send_c, relay, edge, halo_out, halo_in, bands,
     load_sem, tab_sem, a_send, a_recv, b_send, b_recv, g_send, g_recv, c_send, c_recv, h_send, h_recv, out_sem,
 ):
     me_s = lax.axis_index("strip")
@@ -49,6 +48,7 @@
     lb = me_c // 2
     rh = lax.rem(me_c, 2)
     levels, filt = taps.shape
+    reach = (filt - 1) * 2 ** (levels - 1)
     ring = strips // 2
     xring = chans // 4
 
@@ -105,11 +105,15 @@
         xs[c * wide : c * wide + rows, :] = im
         xs[c * wide + rows : (c + 1) * wide, :] = -re
 
-    def a_src(k, j):
-        return send_a.at[j * rows : (j + 1) * rows, k * wide : (k + 1) * wide]
-
-    def a_dst(k, j):
-        return recv_a.at[k, :, partner[j] * wide : (partner[j] + 1) * wide]
+    pieces = [(k, 0, rows) for k in range(local - 1)] + [(local - 1, 0, half), (local - 1, half, rows)]
+
+    def a_src(p, j):
+        k, top, end = pieces[p]
+        return send_a.at[j * rows + top : j * rows + end, k * wide : (k + 1) * wide]
+
+    def a_dst(p, j):
+        k, top, end = pieces[p]
+        return recv_a.at[k, top:end, partner[j] * wide : (partner[j] + 1) * wide]
 
     def a_remote(k, j):
         return pltpu.make_async_remote_copy(
@@ -120,6 +124,31 @@
     def a_local(k):
         last = strips - 1
         return pltpu.make_async_copy(a_src(k, last), a_dst(k, last), a_recv.at[k, nblk - 1])
+
+    load_model.wait()
+    for c in range(local):
+        value = m_v[c]
+        top = value.astype(BF16)
+        own_hi[c] = top
+        own_lo[c] = (value - top.astype(F32)).astype(BF16)
+        edge[0, c * reach : (c + 1) * reach] = m_v[c, rows - reach :]
+        edge[1, c * reach : (c + 1) * reach] = m_v[c, :reach]
+    halo_out[...] = edge[...].astype(BF16)
+    bit = lax.rem(me_s, 2)
+    part = side // 2
+    pair = 1 - 2 * bit
+
+    def leg(i, src, dst, to):
+        return pltpu.make_async_remote_copy(
+            src_ref=src, dst_ref=dst, send_sem=h_send.at[i], recv_sem=h_recv.at[i],
+            device_id=(strip_next(to), me_c), device_id_type=MESH,
+        )
+
+    legs = [
+        leg(0, halo_out.at[bit], halo_in.at[bit], pair),
+        leg(1, halo_out.at[1 - bit, :, :part], halo_in.at[1 - bit, :, :part], -pair),
+        leg(2, halo_out.at[1 - bit, :, part:], relay, pair),
+    ]
 
     for i in range(nblk):
         tab_wait(i)
@@ -130,61 +159,53 @@
         send_a[4 * i * rows : 4 * (i + 1) * rows, :] = value.astype(BF16)
         if i == 0:
             pl.semaphore_wait(barrier, strips - 1 + chans - 1)
+            for i_leg in (2, 0, 1):
+                legs[i_leg].start()
 
         for j in range(4 * i, min(4 * i + 4, strips - 1)):
             a_remote(0, j).start()
 
     a_local(0).start()
 
-    load_model.wait()
-    ext_hi[:, rows + 2 * HALO :, :] = jnp.zeros((local, 128 - rows - 2 * HALO, side), BF16)
-    ext_lo[:, :HALO, :] = jnp.zeros((local, HALO, side), BF16)
-    ext_lo[:, rows + HALO :, :] = jnp.zeros((local, 128 - rows - HALO, side), BF16)
-    for c in range(local):
-        value = m_v[c]
-        top = value.astype(BF16)
-        ext_hi[c, HALO : HALO + rows, :] = top
-        ext_lo[c, HALO : HALO + rows, :] = (value - top.astype(F32)).astype(BF16)
-    halo_copies = [
-        pltpu.make_async_remote_copy(
-            src_ref=ext_hi.at[:, rows : rows + HALO, :], dst_ref=ext_hi.at[:, 0:HALO, :],
-            send_sem=h_send.at[0], recv_sem=h_recv.at[0],
-            device_id=(strip_next(1), me_c), device_id_type=MESH,
-        ),
-        pltpu.make_async_remote_copy(
-            src_ref=ext_hi.at[:, HALO : 2 * HALO, :], dst_ref=ext_hi.at[:, rows + HALO : rows + 2 * HALO, :],
-            send_sem=h_send.at[1], recv_sem=h_recv.at[1],
-            device_id=(strip_next(-1), me_c), device_id_type=MESH,
-        ),
-    ]
-    for cp in halo_copies:
-        cp.start()
-
-    for k in range(1, local):
+    for j in range(strips - 1):
+        a_remote(1, j).start()
+    a_local(1).start()
+    legs[2].wait_recv()
+    leg(3, relay, halo_in.at[bit, :, part:], 2 * pair).start()
+    for k in range(2, local + 1):
         for j in range(strips - 1):
             a_remote(k, j).start()
-
         a_local(k).start()
 
-    row = lax.broadcasted_iota(jnp.int32, (rows, 128), 0)
-    col = lax.broadcasted_iota(jnp.int32, (rows, 128), 1)
-    shift = col - row - HALO
     total = strips * rows
     base_row = me_s * rows
-    band = jnp.zeros((rows, 128), F32)
-    for j in range(levels):
-        dil = 2**j
-        for k in range(filt):
-            inner = jnp.zeros((rows, 128), F32)
-            for q in range(filt):
-                inner = inner + jnp.where(shift == (q - k) * dil, taps[j, q], 0.0)
-            detail_row = base_row + row - (k - filt // 2) * dil
-            ok = jnp.logical_and(detail_row >= 0, detail_row < total)
-            band = band + jnp.where(ok, taps[j, k] * inner, 0.0)
-    image_row = base_row + col - HALO
-    band = jnp.where(jnp.logical_and(image_row >= 0, image_row < total), band, 0.0)
-    band_hi = band.astype(BF16)
-    band_lo = (band - band_hi.astype(F32)).astype(BF16)
+    row = lax.broadcasted_iota(jnp.int32, (rows, 256), 0)
+    col = lax.broadcasted_iota(jnp.int32, (rows, 256), 1)
+    for c in range(local):
+        before = col - rows - c * reach
+        after = before - local * reach
+        own = col < rows
+        in_before = jnp.logical_and(before >= 0, before < reach)
+        in_after = jnp.logical_and(after >= 0, after < reach)
+        place = jnp.where(own, col, jnp.where(in_before, before - reach, rows + after))
+        shift = place - row
+        band = jnp.zeros((rows, 256), F32)
+        for j in range(levels):
+            dil = 2**j
+            for k in range(filt):
+                inner = jnp.zeros((rows, 256), F32)
+                for q in range(filt):
+                    inner = inner + jnp.where(shift == (q - k) * dil, taps[j, q], 0.0)
+                detail_row = base_row + row - (k - filt // 2) * dil
+                ok = jnp.logical_and(detail_row >= 0, detail_row < total)
+                band = band + jnp.where(ok, taps[j, k] * inner, 0.0)
+        image_row = base_row + place
+        known = jnp.logical_or(own, jnp.logical_or(in_before, in_after))
+        known = jnp.logical_and(known, jnp.logical_and(image_row >= 0, image_row < total))
+        band = jnp.where(known, band, 0.0)
+        band_hi = band.astype(BF16)
+        bands[c, 0] = band_hi
+        bands[c, 1] = (band - band_hi.astype(F32)).astype(BF16)
     x[...] = jnp.zeros(x.shape, BF16)
     def b_src(k, peer):
         return send_b.at[
@@ -198,36 +219,50 @@
         )
 
     def wavelet():
-        for cp in halo_copies:
-            cp.wait_recv()
+        for ref, i in ((halo_in.at[0], 0), (relay, 1), (relay, 3)):
+            pltpu.make_async_copy(ref, ref, h_recv.at[i]).wait()
+        filler = jnp.zeros((256 - rows - 2 * local * reach, side), BF16)
         for c in range(local):
-            near = ext_hi[c]
-            wav = jnp.dot(band_hi, near, preferred_element_type=F32)
-            wav = wav + jnp.dot(band_hi, ext_lo[c], preferred_element_type=F32)
-            wav = wav + jnp.dot(band_lo, near, preferred_element_type=F32)
+            near = jnp.concatenate((own_hi[c], halo_in[0], halo_in[1], filler), axis=0)
+            wav = jnp.dot(bands[c, 0], near, preferred_element_type=F32)
+            wav = wav + jnp.dot(bands[c, 0, :, :rows], own_lo[c], preferred_element_type=F32)
+            wav = wav + jnp.dot(bands[c, 1], near, preferred_element_type=F32)
             m_v[c] = m_v[c] - step[c] * wav
 
-    def arrive_a(k):
+    def arrive_a(p):
+        k, top, end = pieces[p]
         for g in range(nblk):
             span = 4 * wide
-            part = recv_a.at[k, :, g * span : (g + 1) * span]
-            pltpu.make_async_copy(part, part, a_recv.at[k, g]).wait()
+            part = recv_a.at[k, top:end, g * span : (g + 1) * span]
+            pltpu.make_async_copy(part, part, a_recv.at[p, g]).wait()
             dirty = jnp.dot(
-                recv_a[k, :, g * span : (g + 1) * span], tb[4 * g : 4 * g + 4].reshape(span, side),
+                recv_a[k, top:end, g * span : (g + 1) * span], tb[4 * g : 4 * g + 4].reshape(span, side),
                 preferred_element_type=F32,
             )
-            base[k] = base[k] + dirty if g else dirty
-
-    def depart_b(k):
-        value = m_v[k] + step[k] * base[k]
-        base[k] = value
-        send_b[k] = value.astype(BF16)
-
-        for peer in peers:
-            b_remote(k, peer).start()
-
-        pltpu.make_async_copy(b_src(k, me_c), recv_b.at[k, me_c], b_recv.at[k]).start()
-        pltpu.make_async_copy(base.at[k], moved.at[k], out_sem).start()
+            base[k, top:end] = base[k, top:end] + dirty if g else dirty
+
+    def depart_b(p):
+        k, top, end = pieces[p]
+        value = m_v[k, top:end] + step[k] * base[k, top:end]
+        base[k, top:end] = value
+        send_b[k, top:end] = value.astype(BF16)
+        pltpu.make_async_copy(base.at[k, top:end], moved.at[k, top:end], out_sem).start()
+        if end - top == rows:
+            for peer in peers:
+                b_remote(k, peer).start()
+            pltpu.make_async_copy(b_src(k, me_c), recv_b.at[k, me_c], b_recv.at[k]).start()
+            return
+        core = top // half
+        for j in range(0, chans - 2, 2):
+            b_remote(k, p_bit[1 - j // 2 % 2] + x_of[xsteps[j // 4]] + core).start()
+
+        @pl.when(rh == core)
+        def _():
+            pltpu.make_async_copy(b_src(k, me_c), recv_b.at[k, me_c], b_recv.at[k]).start()
+
+        @pl.when(rh != core)
+        def _():
+            b_remote(k, peers[-1]).start()
 
     def g_remote(k, peer):
         return pltpu.make_async_remote_copy(
@@ -260,6 +295,8 @@
         arrive_b(k)
     arrive_a(last)
     depart_b(last)
+    arrive_a(last + 1)
+    depart_b(last + 1)
     arrive_b(last - 1)
     arrive_b(last)
 
@@ -316,8 +353,8 @@
     pltpu.make_async_copy(base, moved, out_sem).wait()
     pltpu.make_async_copy(polar, polar, c_recv).wait()
 
-    for cp in halo_copies:
-        cp.wait_send()
+    for ref, i in ((halo_out.at[0], 0), (relay, 1), (relay, 2), (relay, 3)):
+        pltpu.make_async_copy(ref, ref, h_send.at[i]).wait()
     for ref, sem in (
         (send_a.at[: (strips - 1) * rows], a_send),
         (recv_b.at[:, : chans - 1], b_send),
@@ -334,6 +371,7 @@
         local, rows, side = model.shape
         wide = 2 * rows
         half = rows // 2
+        reach = (taps.shape[1] - 1) * 2 ** (taps.shape[0] - 1)
         tab = make_tables(side, strips)
         dma = pltpu.SemaphoreType.DMA
         anywhere = pl.BlockSpec(memory_space=pl.ANY)
@@ -354,8 +392,8 @@
                 pltpu.VMEM((local * wide, side), BF16),
                 pltpu.VMEM((side, local * wide), BF16),
                 pltpu.VMEM((local, rows, strips * wide), BF16),
-                pltpu.VMEM((local, 128, side), BF16),
-                pltpu.VMEM((local, 128, side), BF16),
+                pltpu.VMEM((local, rows, side), BF16),
+                pltpu.VMEM((local, rows, side), BF16),
                 pltpu.VMEM((local, rows, side), F32),
                 pltpu.VMEM((local, rows, side), BF16),
                 pltpu.VMEM((local, chans, half, 128), BF16),
@@ -363,12 +401,17 @@
                 pltpu.VMEM((local, chans, chans // 2, 128), F32),
                 pltpu.VMEM((local * chans * half // 2, 128), F32),
                 pltpu.VMEM((2, chans, local, half // 2, 128), BF16),
+                pltpu.VMEM((local * reach, side // 2), BF16),
+                pltpu.VMEM((2, local * reach, side), F32),
+                pltpu.VMEM((2, local * reach, side), BF16),
+                pltpu.VMEM((2, local * reach, side), BF16),
+                pltpu.VMEM((local, 2, rows, 256), BF16),
                 dma((2,)), dma((strips // 4,)),
-                dma, dma((local, strips // 4)),
+                dma, dma((local + 1, strips // 4)),
                 dma, dma((local,)),
                 dma, dma((local,)),
                 dma, dma,
-                dma((2,)), dma((2,)), dma,
+                dma((4,)), dma((4,)), dma,
             ],
             compiler_params=pltpu.CompilerParams(
                 collective_id=0, has_side_effects=True, vmem_limit_bytes=60 * 1024 * 1024

time: 61.6 us -> 60.8 us (0.987)
  Pallas kernels: 59.7 us -> 58.9 us
    pallas_call x1, Pallas kernels: 59.7 us -> 58.9 us  [step_fn(): pl.pallas_call(functools.partial(kernel, strips, chans), out_shape=(pltpu...]
where the time goes in v3:
time: 60.8 us; the launch traced here: 60.7 us
  Pallas kernels  58.9 us (97%)
  other arithmetic  1.16 us (2%)
  between operations  0.66 us (1%)
    pallas_call x1, Pallas kernels, step_fn(): pl.pallas_call(functools.partial(kernel, strips, chans), out_shape=(pltpu...  58.9 us

profile of v3, /device:TPU:1, one launch (start us, length us, event | category | flops | bytes accessed | tf_op | source)
XLA Modules:
  0.0 60.7 jit_solution(13999495830405405154)
XLA Ops:
  0.7 58.9 %imaging_step.1 = (f32[4,64,1024]{2,1,0:T(8,128)S(1)}, bf16[4,64,1024]{2,1,0:T(8,128)(2,1)S(1)}) custom-call(bf16[16,2,64,1024]{3,2,1,0:T(8,128)(2,1)} %constant.2.clone.tab, bf16[2,4,64,1024]{3,2,1,0:T(8,128)(2,1)} %grid.1, f32[4,64,1024]{2,1,0:T(8,128)} %model.1, f32[4]{0:T(128)} %step.1, f32[3,4]{1,0:T(4,128)} %taps.1, f32[1]{0:T(128)S(6)} %copy.7.shrink), custom_call_target="tpu_custom_call" | custom-call | tf_op jit(solution)/shard_map/imaging_step/pallas_call | solution.py:379
  59.5 1.2 %convert_subtract_fusion = f32[4,64,1024]{2,1,0:T(8,128)} fusion(f32[4,64,1024]{2,1,0:T(8,128)S(1)} %get-tuple-element.7, bf16[4,64,1024]{2,1,0:T(8,128)(2,1)S(1)} %get-tuple-element.8), kind=kLoop, calls=%fused_computation | loop fusion | flops 524288 | bytes 2621440 | tf_op jit(solution)/shard_map/sub | solution.py:421

commit v4 on v3

--- a/solution.py
+++ b/solution.py
@@ -291,14 +291,11 @@
             depart_b(0)
         if k:
             depart_b(k)
-    for k in range(last - 1):
+    for p in range(last, len(pieces)):
+        arrive_a(p)
+        depart_b(p)
+    for k in range(local):
         arrive_b(k)
-    arrive_a(last)
-    depart_b(last)
-    arrive_a(last + 1)
-    depart_b(last + 1)
-    arrive_b(last - 1)
-    arrive_b(last)
 
     blocks = []
     for k in range(local):

time: 60.8 us -> 60.7 us (level)
  no operation moved by 1% of the time
where the time goes in v4:
time: 60.7 us; the launch traced here: 60.6 us
  Pallas kernels  58.7 us (97%)
  other arithmetic  1.16 us (2%)
  between operations  0.66 us (1%)
    pallas_call x1, Pallas kernels, step_fn(): pl.pallas_call(functools.partial(kernel, strips, chans), out_shape=(pltpu...  58.7 us

profile of v4, /device:TPU:1, one launch (start us, length us, event | category | flops | bytes accessed | tf_op | source)
XLA Modules:
  0.0 60.6 jit_solution(1627199895905541457)
XLA Ops:
  0.7 58.7 %imaging_step.1 = (f32[4,64,1024]{2,1,0:T(8,128)S(1)}, bf16[4,64,1024]{2,1,0:T(8,128)(2,1)S(1)}) custom-call(bf16[16,2,64,1024]{3,2,1,0:T(8,128)(2,1)} %constant.2.clone.tab, bf16[2,4,64,1024]{3,2,1,0:T(8,128)(2,1)} %grid.1, f32[4,64,1024]{2,1,0:T(8,128)} %model.1, f32[4]{0:T(128)} %step.1, f32[3,4]{1,0:T(4,128)} %taps.1, f32[1]{0:T(128)S(6)} %copy.7.shrink), custom_call_target="tpu_custom_call" | custom-call | tf_op jit(solution)/shard_map/imaging_step/pallas_call | solution.py:376
  59.4 1.2 %convert_subtract_fusion = f32[4,64,1024]{2,1,0:T(8,128)} fusion(f32[4,64,1024]{2,1,0:T(8,128)S(1)} %get-tuple-element.7, bf16[4,64,1024]{2,1,0:T(8,128)(2,1)S(1)} %get-tuple-element.8), kind=kLoop, calls=%fused_computation | loop fusion | flops 524288 | bytes 2621440 | tf_op jit(solution)/shard_map/sub | solution.py:418

commit v5 on v4

--- a/solution.py
+++ b/solution.py
@@ -125,6 +125,21 @@
         last = strips - 1
         return pltpu.make_async_copy(a_src(k, last), a_dst(k, last), a_recv.at[k, nblk - 1])
 
+    for i in range(nblk):
+        tab_wait(i)
+        cos_rows = tb[4 * i : 4 * i + 4, 0].reshape(4 * rows, side)
+        sin_rows = tb[4 * i : 4 * i + 4, 1].reshape(4 * rows, side)
+        value = lax.dot_general(cos_rows, xc[...], NT, preferred_element_type=F32)
+        value = value + lax.dot_general(sin_rows, xs[...], NT, preferred_element_type=F32)
+        send_a[4 * i * rows : 4 * (i + 1) * rows, :] = value.astype(BF16)
+        if i == 0:
+            pl.semaphore_wait(barrier, strips - 1 + chans - 1)
+
+        for j in range(4 * i, min(4 * i + 4, strips - 1)):
+            a_remote(0, j).start()
+
+    a_local(0).start()
+
     load_model.wait()
     for c in range(local):
         value = m_v[c]
@@ -149,23 +164,8 @@
         leg(1, halo_out.at[1 - bit, :, :part], halo_in.at[1 - bit, :, :part], -pair),
         leg(2, halo_out.at[1 - bit, :, part:], relay, pair),
     ]
-
-    for i in range(nblk):
-        tab_wait(i)
-        cos_rows = tb[4 * i : 4 * i + 4, 0].reshape(4 * rows, side)
-        sin_rows = tb[4 * i : 4 * i + 4, 1].reshape(4 * rows, side)
-        value = lax.dot_general(cos_rows, xc[...], NT, preferred_element_type=F32)
-        value = value + lax.dot_general(sin_rows, xs[...], NT, preferred_element_type=F32)
-        send_a[4 * i * rows : 4 * (i + 1) * rows, :] = value.astype(BF16)
-        if i == 0:
-            pl.semaphore_wait(barrier, strips - 1 + chans - 1)
-            for i_leg in (2, 0, 1):
-                legs[i_leg].start()
-
-        for j in range(4 * i, min(4 * i + 4, strips - 1)):
-            a_remote(0, j).start()
-
-    a_local(0).start()
+    for i in (2, 0, 1):
+        legs[i].start()
 
     for j in range(strips - 1):
         a_remote(1, j).start()

time: 60.7 us -> 59.7 us (0.984)
  Pallas kernels: 58.7 us -> 57.8 us
    pallas_call x1, Pallas kernels: 58.7 us -> 57.8 us  [step_fn(): pl.pallas_call(functools.partial(kernel, strips, chans), out_shape=(pltpu...]
where the time goes in v5:
time: 59.7 us; the launch traced here: 59.6 us
  Pallas kernels  57.8 us (97%)
  other arithmetic  1.16 us (2%)
  between operations  0.66 us (1%)
    pallas_call x1, Pallas kernels, step_fn(): pl.pallas_call(functools.partial(kernel, strips, chans), out_shape=(pltpu...  57.8 us

profile of v5, /device:TPU:1, one launch (start us, length us, event | category | flops | bytes accessed | tf_op | source)
XLA Modules:
  0.0 59.6 jit_solution(9365997804861786095)
XLA Ops:
  0.7 57.8 %imaging_step.1 = (f32[4,64,1024]{2,1,0:T(8,128)S(1)}, bf16[4,64,1024]{2,1,0:T(8,128)(2,1)S(1)}) custom-call(bf16[16,2,64,1024]{3,2,1,0:T(8,128)(2,1)} %constant.2.clone.tab, bf16[2,4,64,1024]{3,2,1,0:T(8,128)(2,1)} %grid.1, f32[4,64,1024]{2,1,0:T(8,128)} %model.1, f32[4]{0:T(128)} %step.1, f32[3,4]{1,0:T(4,128)} %taps.1, f32[1]{0:T(128)S(6)} %copy.7.shrink), custom_call_target="tpu_custom_call" | custom-call | tf_op jit(solution)/shard_map/imaging_step/pallas_call | solution.py:376
  58.4 1.2 %convert_subtract_fusion = f32[4,64,1024]{2,1,0:T(8,128)} fusion(f32[4,64,1024]{2,1,0:T(8,128)S(1)} %get-tuple-element.7, bf16[4,64,1024]{2,1,0:T(8,128)(2,1)S(1)} %get-tuple-element.8), kind=kLoop, calls=%fused_computation | loop fusion | flops 524288 | bytes 2621440 | tf_op jit(solution)/shard_map/sub | solution.py:418
